TPU v7x, 256 devices: a whole 4x4x8 slice. The times are simulated.
256 devices in a mesh: ha: 16 (over x, y_hi, core), wa: 16 (over z, y_lo).
Axes of the slice: x: 4, y: 4 (y_hi: 2, y_lo: 2; y = y_hi * 2 + y_lo), z: 8, core: 2. Of those that a mesh axis runs over, the one named last changes fastest.
Arguments:
- tokens: bfloat16 [256, 256, 256], P('ha', 'wa'), may hold values from -6 to 6
- gain_attn: float32 [256], replicated, may hold values from 0.25 to 1.75
- qkv_fine: bfloat16 [256, 768], replicated, may hold values from -0.375 to 0.375
- scale_fine: float32 [4], replicated, may hold values from 2 to 24
- out_fine: bfloat16 [256, 256], replicated, may hold values from -0.375 to 0.375
- gain_ffn: float32 [256], replicated, may hold values from 0.25 to 1.75
- ffn_in: bfloat16 [256, 1536], replicated, may hold values from -0.375 to 0.375
- ffn_out: bfloat16 [768, 256], replicated, may hold values from -0.21875 to 0.21875
- up_proj: bfloat16 [256, 1024], replicated, may hold values from -0.375 to 0.375
- gain_coarse: float32 [1024], replicated, may hold values from 0.25 to 1.75
- qkv_coarse: bfloat16 [1024, 3072], replicated, may hold values from -0.1875 to 0.1875
- scale_coarse: float32 [16], replicated, may hold values from 2 to 24
- out_coarse: bfloat16 [1024, 1024], replicated, may hold values from -0.1875 to 0.1875
Outputs:
- fine_out: bfloat16 [256, 256, 256], P('ha', 'wa')
- coarse_out: bfloat16 [16, 16, 1024], P('ha', 'wa')
All inputs are finite; a program needn't handle non-finite values.
Results may differ from a plain program's by a relative error of at most 0.03.
Values may be sent and summed in bfloat16 or wider, within the bound.
A program may use at most 128 MiB of HBM per device.

v0:
```python
import jax
import jax.numpy as jnp
from jax import lax
from jax.sharding import PartitionSpec as P

CC = 1024
HD = 64
FFH = 768
RADIUS = 3
POOL = 16


def with_halo(cells, sides, width):
    for axis, dim in sides:
        count = lax.axis_size(axis)
        ends = count - 1
        head = lax.slice_in_dim(cells, 0, width, axis=dim)
        tail = lax.slice_in_dim(cells, cells.shape[dim] - width, cells.shape[dim], axis=dim)
        cells = jnp.concatenate(
            [
                lax.ppermute(tail, axis, [(i, (i + 1) % count) for i in range(ends)]),
                cells,
                lax.ppermute(head, axis, [((i + 1) % count, i) for i in range(ends)]),
            ],
            axis=dim,
        )
    return cells


def rms_scale(values, gain):
    values = values.astype(jnp.float32)
    return values * lax.rsqrt(jnp.mean(values * values, -1, keepdims=True) + 1e-06) * gain


def head_norm(values, heads):
    shaped = values.reshape(values.shape[:-1] + (heads, HD))
    return shaped * lax.rsqrt(jnp.mean(shaped * shaped, -1, keepdims=True) + 1e-06)


def attend_all(queries, keys_all, values_all, scales):
    cscores = (
        jnp.einsum("qhd,khd->hqk", queries, keys_all, preferred_element_type=jnp.float32)
        * (scales / HD)[:, None, None]
    )
    ctop = jnp.max(cscores, -1, keepdims=True)
    cexp = jnp.exp(cscores - ctop)
    cweights = (cexp / jnp.sum(cexp, -1, keepdims=True)).astype(jnp.bfloat16)
    return jnp.einsum(
        "hqk,khd->qhd", cweights, values_all, preferred_element_type=jnp.float32
    ).astype(jnp.bfloat16)


def shards(
    tokens,
    gain_attn,
    qkv_fine,
    scale_fine,
    out_fine,
    gain_ffn,
    ffn_in,
    ffn_out,
    up_proj,
    gain_coarse,
    qkv_coarse,
    scale_coarse,
    out_coarse,
):
    rows, cols, width = tokens.shape
    heads = width // HD
    count = rows * cols
    normed = rms_scale(tokens, gain_attn).astype(jnp.bfloat16).reshape(count, width)
    proj = jnp.dot(normed, qkv_fine, preferred_element_type=jnp.float32).reshape(
        rows, cols, 3 * width
    )
    query = head_norm(proj[..., :width], heads).astype(jnp.bfloat16).reshape(count, heads, HD)
    key_flat = head_norm(proj[..., width : 2 * width], heads).reshape(rows, cols, width)
    pairs = jnp.concatenate([key_flat, proj[..., 2 * width :]], -1).astype(jnp.bfloat16)
    padded = with_halo(pairs, (("ha", 0), ("wa", 1)), RADIUS)
    row_ids = lax.axis_index("ha") * rows + jnp.arange(rows + 2 * RADIUS, dtype=jnp.int32) - RADIUS
    col_ids = lax.axis_index("wa") * cols + jnp.arange(cols + 2 * RADIUS, dtype=jnp.int32) - RADIUS
    row_ok = (row_ids >= 0) & (row_ids < rows * lax.axis_size("ha"))
    col_ok = (col_ids >= 0) & (col_ids < cols * lax.axis_size("wa"))
    valid = row_ok[:, None] & col_ok[None, :]
    span = 2 * RADIUS + 1
    key_list = []
    value_list = []
    valid_list = []
    for shift_a in range(span):
        for shift_b in range(span):
            window = padded[shift_a : shift_a + rows, shift_b : shift_b + cols]
            key_list.append(window[..., :width])
            value_list.append(window[..., width:])
            valid_list.append(valid[shift_a : shift_a + rows, shift_b : shift_b + cols])
    key_stack = jnp.stack(key_list).reshape(span * span, count, heads, HD)
    value_stack = jnp.stack(value_list).reshape(span * span, count, heads, HD)
    valid_stack = jnp.stack(valid_list).reshape(span * span, count)
    raw = (
        jnp.einsum("nhd,snhd->hsn", query, key_stack, preferred_element_type=jnp.float32)
        * (scale_fine / HD)[:, None, None]
    )
    scores = jnp.where(valid_stack[None], raw, -1e30)
    top = jnp.max(scores, 1, keepdims=True)
    expo = jnp.exp(scores - top)
    weights = (expo / jnp.sum(expo, 1, keepdims=True)).astype(jnp.bfloat16)
    attn = jnp.einsum("hsn,snhd->nhd", weights, value_stack, preferred_element_type=jnp.float32)
    attn = attn.astype(jnp.bfloat16).reshape(count, width)
    h1 = (
        tokens.reshape(count, width).astype(jnp.float32)
        + jnp.dot(attn, out_fine, preferred_element_type=jnp.float32)
    ).astype(jnp.bfloat16)
    n2 = rms_scale(h1, gain_ffn).astype(jnp.bfloat16)
    mixed = jnp.dot(n2, ffn_in, preferred_element_type=jnp.float32)
    gated = (jax.nn.gelu(mixed[:, :FFH], approximate=True) * mixed[:, FFH:]).astype(jnp.bfloat16)
    fine_out = (
        h1.astype(jnp.float32) + jnp.dot(gated, ffn_out, preferred_element_type=jnp.float32)
    ).astype(jnp.bfloat16)
    fine_out = fine_out.reshape(rows, cols, width)
    rows_c, cols_c = (rows // POOL, cols // POOL)
    pooled = (
        fine_out.astype(jnp.float32).reshape(rows_c, POOL, cols_c, POOL, width).mean(axis=(1, 3))
    )
    pooled = pooled.astype(jnp.bfloat16).reshape(rows_c * cols_c, width)
    heads_c = CC // HD
    coarse = jnp.dot(pooled, up_proj, preferred_element_type=jnp.float32).astype(jnp.bfloat16)
    ncoarse = rms_scale(coarse, gain_coarse).astype(jnp.bfloat16)
    pc = jnp.dot(ncoarse, qkv_coarse, preferred_element_type=jnp.float32)
    cq = head_norm(pc[:, :CC], heads_c).astype(jnp.bfloat16)
    local_kv = jnp.concatenate(
        [head_norm(pc[:, CC : 2 * CC], heads_c).reshape(-1, CC), pc[:, 2 * CC :]], -1
    ).astype(jnp.bfloat16)
    all_kv = lax.all_gather(local_kv, ("ha", "wa"), axis=0, tiled=True)
    ck = all_kv[:, :CC].reshape(-1, heads_c, HD)
    cv = all_kv[:, CC:].reshape(-1, heads_c, HD)
    cattn = attend_all(cq, ck, cv, scale_coarse).reshape(-1, CC)
    coarse_out = (
        coarse.astype(jnp.float32) + jnp.dot(cattn, out_coarse, preferred_element_type=jnp.float32)
    ).astype(jnp.bfloat16)
    return (fine_out, coarse_out.reshape(rows_c, cols_c, CC))


def solution(mesh):
    return jax.shard_map(
        shards,
        mesh=mesh,
        in_specs=(P("ha", "wa", None), P(), P(), P(), P(), P(), P(), P(), P(), P(), P(), P(), P()),
        out_specs=(P("ha", "wa", None), P("ha", "wa", None)),
        check_vma=False,
    )
```

profile of v0, /device:TPU:99, one launch (start us, length us, event | category | flops | bytes accessed | tf_op | source)
XLA Modules:
  0.0 1168.6 jit_solution(1315303001375330019)
XLA Ops:
  13.5 2.1 mul.205
  17.9 2.6 collective-permute-start.1
  20.5 4.7 collective-permute-start
  68.9 2.5 collective-permute-start.3
  71.4 3.3 collective-permute-start.2
  76.5 1.8 stack.503
  100.1 1.8 stack.501
  101.9 1.8 stack.502
  103.7 1.8 stack.504
  107.2 1.8 stack.506
  112.6 1.8 stack.509
  114.4 1.8 stack.511
  118.0 1.8 stack.513
  119.8 1.8 stack.514
  121.6 1.8 stack.515
  123.4 1.8 stack.516
  132.2 1.8 stack.522
  134.0 1.8 stack.523
  137.6 1.8 stack.526
  139.4 1.8 stack.527
  141.2 1.8 stack.528
  144.8 1.8 stack.530
  146.6 1.8 stack.532
  148.4 1.8 stack.533
  155.5 1.8 stack.537
  159.1 1.8 stack.540
  162.7 1.8 stack.542
  168.0 1.8 stack.546
  171.6 1.8 stack.548
  173.6 1.9 constant_dynamic-update-slice_fusion.47
  189.5 1.9 constant_dynamic-update-slice_fusion.38
  234.9 23.5 %fusion = f32[4,256,1,49]{3,2,1,0:T(1,128)} fusion(bf16[49,256,4,64]{3,2,1,0:T(4,128)(2,1)} %constant_dynamic-update-slice_fusion, bf16[256,4,64,1]{2,1,0,3:T(4,128)(2,1)S(1)} %copy-done.48), kind=kOutput, calls=%fused_computation.1 | convolution fusion | flops 6422528 | bytes 6754304 | tf_op jit(solution)/shard_map/nhd,snhd->hsn/dot_general | solution.py:98
  260.9 5.2 copy.36
  266.1 1.8 stack.550
  271.5 1.8 stack.552
  273.3 1.8 stack.554
  278.6 1.8 stack.557
  282.2 1.8 stack.559
  284.0 1.8 stack.561
  285.8 1.8 stack.562
  287.6 1.8 stack.563
  296.5 1.8 stack.569
  298.3 1.8 stack.570
  300.1 1.8 stack.571
  305.5 1.8 stack.575
  307.3 1.8 stack.576
  309.1 1.8 stack.577
  310.9 1.8 stack.578
  312.7 1.8 stack.579
  314.5 1.8 stack.580
  316.3 1.8 stack.582
  318.1 1.8 stack.583
  319.9 1.8 stack.584
  323.4 1.8 stack.586
  334.1 1.8 stack.593
  336.8 1.8 stack.596
  338.6 1.8 stack.597
  340.4 1.8 stack.598
  342.3 1.9 constant_dynamic-update-slice_fusion.96
  402.8 18.4 %multiply_reduce_fusion = bf16[256,4,64]{2,1,0:T(4,128)(2,1)S(1)} fusion(f32[256,4,49]{1,0,2:T(8,128)} %copy.36, bf16[49,256,4,64]{3,2,1,0:T(4,128)(2,1)} %constant_dynamic-update-slice_fusion.49), kind=kLoop, calls=%fused_computation | loop fusion | flops 9568256 | bytes 6754304
  423.3 2.1 convert_reduce_fusion
  426.9 3.7 fusion.60
  432.0 722.7 %all-gather.3.cloned.1.call-done = bf16[256,1,2048]{2,1,0:T(2,128)(2,1)} async-done(((bf16[1,1,2048]{2,1,0:T(2,128)(2,1)}), bf16[256,1,2048]{2,1,0:T(2,128)(2,1)}) %all-gather.3.cloned.1.call-update) | async-done | bytes 1048592 | tf_op jit(solution)/shard_map/all_gather | solution.py:131
  1154.7 2.2 copy.55
  (381 shorter events, 265.8 us)
Async XLA Ops:
  7.2 1153.1 %copy-start = (bf16[1024,1024]{1,0:T(8,128)(2,1)S(1)}, bf16[1024,1024]{1,0:T(8,128)(2,1)}, u32[]{:S(2)}) copy-start(bf16[1024,1024]{1,0:T(8,128)(2,1)} %param.25) | copy-start | bytes 6291460
  7.2 1147.6 %all-gather.3.cloned.1.call-start = ((), (), s32[]{:S(2)}) async-start(), calls=%async_computation | async-start | bytes 2105344 | tf_op jit(solution)/shard_map/all_gather | solution.py:131
  17.9 49.4 %collective-permute-start.1 = (bf16[3,16,512]{2,1,0:T(8,128)(2,1)}, bf16[3,16,512]{2,1,0:T(8,128)(2,1)}, u32[]{:S(2)}, u32[]{:S(2)}) collective-permute-start(bf16[3,16,512]{2,1,0:T(8,128)(2,1)} %get-tuple-element.113), channel_id=1, source_target_pairs={{16,0},{32,16},{48,32},{64,48},{80,64},{96,80},{112,96},{128,112},... | collective-permute-start | bytes 147464 | tf_op jit(solution)/shard_map/ppermute | solution.py:23
  20.5 46.9 %collective-permute-start = (bf16[3,16,512]{2,1,0:T(8,128)(2,1)}, bf16[3,16,512]{2,1,0:T(8,128)(2,1)}, u32[]{:S(2)}, u32[]{:S(2)}) collective-permute-start(bf16[3,16,512]{2,1,0:T(8,128)(2,1)} %get-tuple-element.112), channel_id=1, source_target_pairs={{0,16},{16,32},{32,48},{48,64},{64,80},{80,96},{96,112},{112,128},... | collective-permute-start | bytes 147464 | tf_op jit(solution)/shard_map/ppermute | solution.py:21
  68.9 20.5 %collective-permute-start.3 = (bf16[22,3,512]{2,1,0:T(4,128)(2,1)}, bf16[22,3,512]{2,1,0:T(4,128)(2,1)}, u32[]{:S(2)}, u32[]{:S(2)}) collective-permute-start(bf16[22,3,512]{2,1,0:T(4,128)(2,1)} %get-tuple-element.96), channel_id=1, source_target_pairs={{1,0},{2,1},{3,2},{4,3},{5,4},{6,5},{7,6},{8,7},{9,8},{10,9},{11,1... | collective-permute-start | bytes 202760 | tf_op jit(solution)/shard_map/ppermute | solution.py:23
  71.4 18.0 %collective-permute-start.2 = (bf16[22,3,512]{2,1,0:T(4,128)(2,1)}, bf16[22,3,512]{2,1,0:T(4,128)(2,1)}, u32[]{:S(2)}, u32[]{:S(2)}) collective-permute-start(bf16[22,3,512]{2,1,0:T(4,128)(2,1)} %get-tuple-element.97), channel_id=1, source_target_pairs={{0,1},{1,2},{2,3},{3,4},{4,5},{5,6},{6,7},{7,8},{8,9},{9,10},{10,1... | collective-permute-start | bytes 202760 | tf_op jit(solution)/shard_map/ppermute | solution.py:21
  112.6 101.5 %copy-start.3 = (bf16[1,256,4,64]{3,2,1,0:T(4,128)(2,1)S(1)}, bf16[1,256,4,64]{3,2,1,0:T(4,128)(2,1)}, u32[]{:S(2)}) copy-start(bf16[1,256,4,64]{3,2,1,0:T(4,128)(2,1)} %stack.524) | copy-start | bytes 393220
  173.4 43.2 %copy-start.46 = (bf16[1,256,4,64]{3,2,1,0:T(4,128)(2,1)S(1)}, bf16[1,256,4,64]{3,2,1,0:T(4,128)(2,1)}, u32[]{:S(2)}) copy-start(bf16[1,256,4,64]{3,2,1,0:T(4,128)(2,1)} %stack.526) | copy-start | bytes 393220
  173.4 44.0 %copy-start.45 = (bf16[1,256,4,64]{3,2,1,0:T(4,128)(2,1)S(1)}, bf16[1,256,4,64]{3,2,1,0:T(4,128)(2,1)}, u32[]{:S(2)}) copy-start(bf16[1,256,4,64]{3,2,1,0:T(4,128)(2,1)} %stack.527) | copy-start | bytes 393220
  173.4 44.8 %copy-start.43 = (bf16[1,256,4,64]{3,2,1,0:T(4,128)(2,1)S(1)}, bf16[1,256,4,64]{3,2,1,0:T(4,128)(2,1)}, u32[]{:S(2)}) copy-start(bf16[1,256,4,64]{3,2,1,0:T(4,128)(2,1)} %stack.528) | copy-start | bytes 393220
  173.4 45.6 %copy-start.41 = (bf16[1,256,4,64]{3,2,1,0:T(4,128)(2,1)S(1)}, bf16[1,256,4,64]{3,2,1,0:T(4,128)(2,1)}, u32[]{:S(2)}) copy-start(bf16[1,256,4,64]{3,2,1,0:T(4,128)(2,1)} %stack.529) | copy-start | bytes 393220
  173.4 46.4 %copy-start.39 = (bf16[1,256,4,64]{3,2,1,0:T(4,128)(2,1)S(1)}, bf16[1,256,4,64]{3,2,1,0:T(4,128)(2,1)}, u32[]{:S(2)}) copy-start(bf16[1,256,4,64]{3,2,1,0:T(4,128)(2,1)} %stack.530) | copy-start | bytes 393220
  173.4 47.2 %copy-start.6 = (bf16[1,256,4,64]{3,2,1,0:T(4,128)(2,1)S(1)}, bf16[1,256,4,64]{3,2,1,0:T(4,128)(2,1)}, u32[]{:S(2)}) copy-start(bf16[1,256,4,64]{3,2,1,0:T(4,128)(2,1)} %stack.531) | copy-start | bytes 393220
  173.4 48.0 %copy-start.36 = (bf16[1,256,4,64]{3,2,1,0:T(4,128)(2,1)S(1)}, bf16[1,256,4,64]{3,2,1,0:T(4,128)(2,1)}, u32[]{:S(2)}) copy-start(bf16[1,256,4,64]{3,2,1,0:T(4,128)(2,1)} %stack.532) | copy-start | bytes 393220
  173.4 48.7 %copy-start.35 = (bf16[1,256,4,64]{3,2,1,0:T(4,128)(2,1)S(1)}, bf16[1,256,4,64]{3,2,1,0:T(4,128)(2,1)}, u32[]{:S(2)}) copy-start(bf16[1,256,4,64]{3,2,1,0:T(4,128)(2,1)} %stack.533) | copy-start | bytes 393220
  173.5 49.5 %copy-start.33 = (bf16[1,256,4,64]{3,2,1,0:T(4,128)(2,1)S(1)}, bf16[1,256,4,64]{3,2,1,0:T(4,128)(2,1)}, u32[]{:S(2)}) copy-start(bf16[1,256,4,64]{3,2,1,0:T(4,128)(2,1)} %stack.534) | copy-start | bytes 393220
  173.5 50.3 %copy-start.31 = (bf16[1,256,4,64]{3,2,1,0:T(4,128)(2,1)S(1)}, bf16[1,256,4,64]{3,2,1,0:T(4,128)(2,1)}, u32[]{:S(2)}) copy-start(bf16[1,256,4,64]{3,2,1,0:T(4,128)(2,1)} %stack.535) | copy-start | bytes 393220
  173.5 51.1 %copy-start.29 = (bf16[1,256,4,64]{3,2,1,0:T(4,128)(2,1)S(1)}, bf16[1,256,4,64]{3,2,1,0:T(4,128)(2,1)}, u32[]{:S(2)}) copy-start(bf16[1,256,4,64]{3,2,1,0:T(4,128)(2,1)} %stack.536) | copy-start | bytes 393220
  173.5 51.9 %copy-start.27 = (bf16[1,256,4,64]{3,2,1,0:T(4,128)(2,1)S(1)}, bf16[1,256,4,64]{3,2,1,0:T(4,128)(2,1)}, u32[]{:S(2)}) copy-start(bf16[1,256,4,64]{3,2,1,0:T(4,128)(2,1)} %stack.537) | copy-start | bytes 393220
  173.5 52.7 %copy-start.5 = (bf16[1,256,4,64]{3,2,1,0:T(4,128)(2,1)S(1)}, bf16[1,256,4,64]{3,2,1,0:T(4,128)(2,1)}, u32[]{:S(2)}) copy-start(bf16[1,256,4,64]{3,2,1,0:T(4,128)(2,1)} %stack.538) | copy-start | bytes 393220
  173.5 53.5 %copy-start.24 = (bf16[1,256,4,64]{3,2,1,0:T(4,128)(2,1)S(1)}, bf16[1,256,4,64]{3,2,1,0:T(4,128)(2,1)}, u32[]{:S(2)}) copy-start(bf16[1,256,4,64]{3,2,1,0:T(4,128)(2,1)} %stack.539) | copy-start | bytes 393220
  173.5 54.3 %copy-start.23 = (bf16[1,256,4,64]{3,2,1,0:T(4,128)(2,1)S(1)}, bf16[1,256,4,64]{3,2,1,0:T(4,128)(2,1)}, u32[]{:S(2)}) copy-start(bf16[1,256,4,64]{3,2,1,0:T(4,128)(2,1)} %stack.540) | copy-start | bytes 393220
  173.5 55.0 %copy-start.21 = (bf16[1,256,4,64]{3,2,1,0:T(4,128)(2,1)S(1)}, bf16[1,256,4,64]{3,2,1,0:T(4,128)(2,1)}, u32[]{:S(2)}) copy-start(bf16[1,256,4,64]{3,2,1,0:T(4,128)(2,1)} %stack.541) | copy-start | bytes 393220
  173.5 55.8 %copy-start.19 = (bf16[1,256,4,64]{3,2,1,0:T(4,128)(2,1)S(1)}, bf16[1,256,4,64]{3,2,1,0:T(4,128)(2,1)}, u32[]{:S(2)}) copy-start(bf16[1,256,4,64]{3,2,1,0:T(4,128)(2,1)} %stack.542) | copy-start | bytes 393220
  173.5 56.6 %copy-start.17 = (bf16[1,256,4,64]{3,2,1,0:T(4,128)(2,1)S(1)}, bf16[1,256,4,64]{3,2,1,0:T(4,128)(2,1)}, u32[]{:S(2)}) copy-start(bf16[1,256,4,64]{3,2,1,0:T(4,128)(2,1)} %stack.543) | copy-start | bytes 393220
  173.6 57.4 %copy-start.15 = (bf16[1,256,4,64]{3,2,1,0:T(4,128)(2,1)S(1)}, bf16[1,256,4,64]{3,2,1,0:T(4,128)(2,1)}, u32[]{:S(2)}) copy-start(bf16[1,256,4,64]{3,2,1,0:T(4,128)(2,1)} %stack.544) | copy-start | bytes 393220
  173.6 58.2 %copy-start.4 = (bf16[1,256,4,64]{3,2,1,0:T(4,128)(2,1)S(1)}, bf16[1,256,4,64]{3,2,1,0:T(4,128)(2,1)}, u32[]{:S(2)}) copy-start(bf16[1,256,4,64]{3,2,1,0:T(4,128)(2,1)} %stack.545) | copy-start | bytes 393220
  173.6 59.0 %copy-start.12 = (bf16[1,256,4,64]{3,2,1,0:T(4,128)(2,1)S(1)}, bf16[1,256,4,64]{3,2,1,0:T(4,128)(2,1)}, u32[]{:S(2)}) copy-start(bf16[1,256,4,64]{3,2,1,0:T(4,128)(2,1)} %stack.546) | copy-start | bytes 393220
  173.6 59.8 %copy-start.10 = (bf16[1,256,4,64]{3,2,1,0:T(4,128)(2,1)S(1)}, bf16[1,256,4,64]{3,2,1,0:T(4,128)(2,1)}, u32[]{:S(2)}) copy-start(bf16[1,256,4,64]{3,2,1,0:T(4,128)(2,1)} %stack.547) | copy-start | bytes 393220
  173.6 60.5 %copy-start.7 = (bf16[1,256,4,64]{3,2,1,0:T(4,128)(2,1)S(1)}, bf16[1,256,4,64]{3,2,1,0:T(4,128)(2,1)}, u32[]{:S(2)}) copy-start(bf16[1,256,4,64]{3,2,1,0:T(4,128)(2,1)} %stack.548) | copy-start | bytes 393220
  173.6 61.3 %copy-start.48 = (bf16[256,4,64,1]{2,1,0,3:T(4,128)(2,1)S(1)}, bf16[256,4,64,1]{2,1,0,3:T(4,128)(2,1)}, u32[]{:S(2)}) copy-start(bf16[256,4,64,1]{2,1,0,3:T(4,128)(2,1)} %fusion.22) | copy-start | bytes 393220
  231.7 28.0 %copy-start.50 = (f32[4]{0:T(128)S(1)}, f32[4]{0:T(128)}, u32[]{:S(2)}) copy-start(f32[4]{0:T(128)} %broadcast_multiply_fusion.1) | copy-start | bytes 52
  266.1 104.3 %copy-start.2 = (bf16[1,256,4,64]{3,2,1,0:T(4,128)(2,1)S(1)}, bf16[1,256,4,64]{3,2,1,0:T(4,128)(2,1)}, u32[]{:S(2)}) copy-start(bf16[1,256,4,64]{3,2,1,0:T(4,128)(2,1)} %stack.567) | copy-start | bytes 393220
  342.2 42.1 %copy-start.44 = (bf16[1,256,4,64]{3,2,1,0:T(4,128)(2,1)S(1)}, bf16[1,256,4,64]{3,2,1,0:T(4,128)(2,1)}, u32[]{:S(2)}) copy-start(bf16[1,256,4,64]{3,2,1,0:T(4,128)(2,1)} %stack.576) | copy-start | bytes 393220
  342.2 42.9 %copy-start.42 = (bf16[1,256,4,64]{3,2,1,0:T(4,128)(2,1)S(1)}, bf16[1,256,4,64]{3,2,1,0:T(4,128)(2,1)}, u32[]{:S(2)}) copy-start(bf16[1,256,4,64]{3,2,1,0:T(4,128)(2,1)} %stack.577) | copy-start | bytes 393220
  342.2 43.7 %copy-start.40 = (bf16[1,256,4,64]{3,2,1,0:T(4,128)(2,1)S(1)}, bf16[1,256,4,64]{3,2,1,0:T(4,128)(2,1)}, u32[]{:S(2)}) copy-start(bf16[1,256,4,64]{3,2,1,0:T(4,128)(2,1)} %stack.578) | copy-start | bytes 393220
  342.2 44.5 %copy-start.38 = (bf16[1,256,4,64]{3,2,1,0:T(4,128)(2,1)S(1)}, bf16[1,256,4,64]{3,2,1,0:T(4,128)(2,1)}, u32[]{:S(2)}) copy-start(bf16[1,256,4,64]{3,2,1,0:T(4,128)(2,1)} %stack.579) | copy-start | bytes 393220
  342.2 45.3 %copy-start.37 = (bf16[1,256,4,64]{3,2,1,0:T(4,128)(2,1)S(1)}, bf16[1,256,4,64]{3,2,1,0:T(4,128)(2,1)}, u32[]{:S(2)}) copy-start(bf16[1,256,4,64]{3,2,1,0:T(4,128)(2,1)} %stack.580) | copy-start | bytes 393220
  342.2 46.9 %copy-start.34 = (bf16[1,256,4,64]{3,2,1,0:T(4,128)(2,1)S(1)}, bf16[1,256,4,64]{3,2,1,0:T(4,128)(2,1)}, u32[]{:S(2)}) copy-start(bf16[1,256,4,64]{3,2,1,0:T(4,128)(2,1)} %stack.582) | copy-start | bytes 393220
  342.2 47.7 %copy-start.32 = (bf16[1,256,4,64]{3,2,1,0:T(4,128)(2,1)S(1)}, bf16[1,256,4,64]{3,2,1,0:T(4,128)(2,1)}, u32[]{:S(2)}) copy-start(bf16[1,256,4,64]{3,2,1,0:T(4,128)(2,1)} %stack.583) | copy-start | bytes 393220
  342.2 48.5 %copy-start.30 = (bf16[1,256,4,64]{3,2,1,0:T(4,128)(2,1)S(1)}, bf16[1,256,4,64]{3,2,1,0:T(4,128)(2,1)}, u32[]{:S(2)}) copy-start(bf16[1,256,4,64]{3,2,1,0:T(4,128)(2,1)} %stack.584) | copy-start | bytes 393220
  342.2 49.3 %copy-start.28 = (bf16[1,256,4,64]{3,2,1,0:T(4,128)(2,1)S(1)}, bf16[1,256,4,64]{3,2,1,0:T(4,128)(2,1)}, u32[]{:S(2)}) copy-start(bf16[1,256,4,64]{3,2,1,0:T(4,128)(2,1)} %stack.585) | copy-start | bytes 393220
  342.2 50.1 %copy-start.26 = (bf16[1,256,4,64]{3,2,1,0:T(4,128)(2,1)S(1)}, bf16[1,256,4,64]{3,2,1,0:T(4,128)(2,1)}, u32[]{:S(2)}) copy-start(bf16[1,256,4,64]{3,2,1,0:T(4,128)(2,1)} %stack.586) | copy-start | bytes 393220
  342.2 50.9 %copy-start.25 = (bf16[1,256,4,64]{3,2,1,0:T(4,128)(2,1)S(1)}, bf16[1,256,4,64]{3,2,1,0:T(4,128)(2,1)}, u32[]{:S(2)}) copy-start(bf16[1,256,4,64]{3,2,1,0:T(4,128)(2,1)} %stack.587) | copy-start | bytes 393220
  342.2 52.5 %copy-start.22 = (bf16[1,256,4,64]{3,2,1,0:T(4,128)(2,1)S(1)}, bf16[1,256,4,64]{3,2,1,0:T(4,128)(2,1)}, u32[]{:S(2)}) copy-start(bf16[1,256,4,64]{3,2,1,0:T(4,128)(2,1)} %stack.589) | copy-start | bytes 393220
  342.3 53.3 %copy-start.20 = (bf16[1,256,4,64]{3,2,1,0:T(4,128)(2,1)S(1)}, bf16[1,256,4,64]{3,2,1,0:T(4,128)(2,1)}, u32[]{:S(2)}) copy-start(bf16[1,256,4,64]{3,2,1,0:T(4,128)(2,1)} %stack.590) | copy-start | bytes 393220
  342.3 54.1 %copy-start.18 = (bf16[1,256,4,64]{3,2,1,0:T(4,128)(2,1)S(1)}, bf16[1,256,4,64]{3,2,1,0:T(4,128)(2,1)}, u32[]{:S(2)}) copy-start(bf16[1,256,4,64]{3,2,1,0:T(4,128)(2,1)} %stack.591) | copy-start | bytes 393220
  342.3 54.9 %copy-start.16 = (bf16[1,256,4,64]{3,2,1,0:T(4,128)(2,1)S(1)}, bf16[1,256,4,64]{3,2,1,0:T(4,128)(2,1)}, u32[]{:S(2)}) copy-start(bf16[1,256,4,64]{3,2,1,0:T(4,128)(2,1)} %stack.592) | copy-start | bytes 393220
  342.3 55.7 %copy-start.13 = (bf16[1,256,4,64]{3,2,1,0:T(4,128)(2,1)S(1)}, bf16[1,256,4,64]{3,2,1,0:T(4,128)(2,1)}, u32[]{:S(2)}) copy-start(bf16[1,256,4,64]{3,2,1,0:T(4,128)(2,1)} %stack.593) | copy-start | bytes 393220
  342.3 56.5 %copy-start.14 = (bf16[1,256,4,64]{3,2,1,0:T(4,128)(2,1)S(1)}, bf16[1,256,4,64]{3,2,1,0:T(4,128)(2,1)}, u32[]{:S(2)}) copy-start(bf16[1,256,4,64]{3,2,1,0:T(4,128)(2,1)} %stack.594) | copy-start | bytes 393220
  342.3 58.1 %copy-start.11 = (bf16[1,256,4,64]{3,2,1,0:T(4,128)(2,1)S(1)}, bf16[1,256,4,64]{3,2,1,0:T(4,128)(2,1)}, u32[]{:S(2)}) copy-start(bf16[1,256,4,64]{3,2,1,0:T(4,128)(2,1)} %stack.596) | copy-start | bytes 393220
  342.3 58.9 %copy-start.8 = (bf16[1,256,4,64]{3,2,1,0:T(4,128)(2,1)S(1)}, bf16[1,256,4,64]{3,2,1,0:T(4,128)(2,1)}, u32[]{:S(2)}) copy-start(bf16[1,256,4,64]{3,2,1,0:T(4,128)(2,1)} %stack.597) | copy-start | bytes 393220
  342.3 59.7 %copy-start.9 = (bf16[1,256,4,64]{3,2,1,0:T(4,128)(2,1)S(1)}, bf16[1,256,4,64]{3,2,1,0:T(4,128)(2,1)}, u32[]{:S(2)}) copy-start(bf16[1,256,4,64]{3,2,1,0:T(4,128)(2,1)} %stack.598) | copy-start | bytes 393220
  394.0 27.4 %copy-start.1 = (bf16[16,16,256]{2,1,0:T(8,128)(2,1)S(1)}, bf16[16,16,256]{2,1,0:T(8,128)(2,1)}, u32[]{:S(2)}) copy-start(bf16[16,16,256]{2,1,0:T(8,128)(2,1)} %param.13) | copy-start | bytes 393220
  394.0 27.4 %copy-start.49 = (bf16[256,256]{1,0:T(8,128)(2,1)S(1)}, bf16[256,256]{1,0:T(8,128)(2,1)}, u32[]{:S(2)}) copy-start(bf16[256,256]{1,0:T(8,128)(2,1)} %param.17) | copy-start | bytes 393220
  394.8 27.0 %copy-start.52 = (f32[256]{0:T(256)S(1)}, f32[256]{0:T(256)}, u32[]{:S(2)}) copy-start(f32[256]{0:T(256)} %param.18) | copy-start | bytes 3076
  402.8 22.6 %copy-start.47 = (bf16[256,1024]{1,0:T(8,128)(2,1)S(1)}, bf16[256,1024]{1,0:T(8,128)(2,1)}, u32[]{:S(2)}) copy-start(bf16[256,1024]{1,0:T(8,128)(2,1)} %param.21) | copy-start | bytes 1572868
  402.8 24.1 %copy-start.51 = (f32[1024]{0:T(1024)S(1)}, f32[1024]{0:T(1024)}, u32[]{:S(2)}) copy-start(f32[1024]{0:T(1024)} %param.22) | copy-start | bytes 12292
  402.8 28.9 %copy-start.53 = (f32[16]{0:T(128)S(1)}, f32[16]{0:T(128)}, u32[]{:S(2)}) copy-start(f32[16]{0:T(128)} %param.24) | copy-start | bytes 196
Sparse Core Ops, SparseCore 0:
  431.8 722.9 all-gather.2
where the time goes:
time: 1180 us; the launch traced here: 1170 us
  waiting for transfers between devices  723 us (61%)
  local copies, waits for them, and re-layouts  349 us (30%)
  matrix products  34.6 us (3%)
  other arithmetic  33.1 us (3%)
  between operations  16 us (1%)
  starting transfers between devices  13.1 us (1%)
    all_gather x1, waiting for transfers between devices, shards(): all_kv = lax.all_gather(local_kv, ('ha', 'wa'), axis=0, tiled=True)  723 us
    unnamed x206, local copies, waits for them, and re-layouts  130 us
    another operation x50, local copies, waits for them, and re-layouts, shards(): key_stack = jnp.stack(key_list).reshape(span * span, count, heads, HD)  85.8 us
    another operation x50, local copies, waits for them, and re-layouts, shards(): value_stack = jnp.stack(value_list).reshape(span * span, count, heads, HD)  78.3 us
    another operation x50, local copies, waits for them, and re-layouts, shards(): valid_stack = jnp.stack(valid_list).reshape(span * span, count)  34.8 us
  transfers between devices with their start and end apart: 5, of which 1 were waited for; matrix products, arithmetic and copies ran while one was open for 5% of the time, Pallas kernels for 0%

commit v1 on v0

--- a/solution.py
+++ b/solution.py
@@ -128,7 +128,10 @@
     local_kv = jnp.concatenate(
         [head_norm(pc[:, CC : 2 * CC], heads_c).reshape(-1, CC), pc[:, 2 * CC :]], -1
     ).astype(jnp.bfloat16)
-    all_kv = lax.all_gather(local_kv, ("ha", "wa"), axis=0, tiled=True)
+    all_kv = jnp.concatenate(
+        lax.all_to_all(jnp.stack([local_kv] * lax.axis_size(("ha", "wa"))), ("ha", "wa"), 0, 0),
+        axis=0,
+    )
     ck = all_kv[:, :CC].reshape(-1, heads_c, HD)
     cv = all_kv[:, CC:].reshape(-1, heads_c, HD)
     cattn = attend_all(cq, ck, cv, scale_coarse).reshape(-1, CC)

time: 1180 us -> 504 us (0.43)
  the two profiles are of different devices: /device:TPU:99 before, /device:TPU:1 now
where the time goes in v1:
time: 504 us; the launch traced here: 496 us
  local copies, waits for them, and re-layouts  357 us (71%)
  other arithmetic  40.6 us (8%)
  matrix products  34.6 us (7%)
  waiting for transfers between devices  31.4 us (6%)
  starting transfers between devices  29.2 us (6%)
    unnamed x208, local copies, waits for them, and re-layouts  136 us
    another operation x50, local copies, waits for them, and re-layouts, shards(): key_stack = jnp.stack(key_list).reshape(span * span, count, heads, HD)  86.1 us
    another operation x50, local copies, waits for them, and re-layouts, shards(): value_stack = jnp.stack(value_list).reshape(span * span, count, heads, HD)  78.2 us
    another operation x50, local copies, waits for them, and re-layouts, shards(): valid_stack = jnp.stack(valid_list).reshape(span * span, count)  34.7 us
    all_to_all x1, waiting for transfers between devices, shards(): lax.all_to_all(jnp.stack([local_kv] * lax.axis_size(('ha', 'wa'))), ('ha'...  31.3 us
    dot_general x1, matrix products, shards(): jnp.einsum('nhd,snhd->hsn', query, key_stack, preferred_element_type=jnp....  23.5 us
    unnamed x2, other arithmetic  19.2 us
    all_to_all x1, starting transfers between devices, shards(): lax.all_to_all(jnp.stack([local_kv] * lax.axis_size(('ha', 'wa'))), ('ha'...  15 us
  transfers between devices with their start and end apart: 5, of which 1 were waited for; matrix products, arithmetic and copies ran while one was open for 12% of the time, Pallas kernels for 0%

profile of v1, /device:TPU:1, one launch (start us, length us, event | category | flops | bytes accessed | tf_op | source)
XLA Modules:
  0.0 495.6 jit_solution(15493275249697088684)
XLA Ops:
  6.9 2.1 mul.205
  11.3 5.1 %collective-permute-start.1 = (bf16[3,16,512]{2,1,0:T(8,128)(2,1)}, bf16[3,16,512]{2,1,0:T(8,128)(2,1)}, u32[]{:S(2)}, u32[]{:S(2)}) collective-permute-start(bf16[3,16,512]{2,1,0:T(8,128)(2,1)} %get-tuple-element.115), channel_id=1, source_target_pairs={{16,0},{32,16},{48,32},{64,48},{80,64},{96,80},{112,96},{128,112},... | collective-permute-start | bytes 147464 | tf_op jit(solution)/shard_map/ppermute | solution.py:23
  16.4 3.0 collective-permute-start
  64.4 4.8 collective-permute-start.2
  78.1 1.8 stack.390
  98.2 1.8 stack.356
  100.0 1.8 stack.357
  101.8 1.8 stack.358
  103.6 1.8 stack.359
  107.2 1.8 stack.361
  112.5 1.8 stack.365
  114.4 1.8 stack.366
  116.2 1.8 stack.367
  117.9 1.8 stack.368
  121.5 1.8 stack.371
  125.1 1.8 stack.373
  126.9 1.8 stack.374
  128.7 1.8 stack.375
  132.3 1.8 stack.378
  137.6 1.8 stack.381
  139.4 1.8 stack.382
  141.2 1.8 stack.384
  143.1 1.8 stack.385
  144.9 1.8 stack.386
  150.2 1.8 stack.389
  152.0 1.8 stack.391
  155.6 1.8 stack.393
  157.4 1.8 stack.394
  159.2 1.8 stack.395
  161.0 1.8 stack.396
  162.8 1.8 stack.398
  164.6 1.8 stack.399
  168.4 1.9 constant_dynamic-update-slice_fusion.47
  184.4 2.2 constant_dynamic-update-slice_fusion.38
  230.3 23.5 %fusion = f32[4,256,1,49]{3,2,1,0:T(1,128)} fusion(bf16[49,256,4,64]{3,2,1,0:T(4,128)(2,1)} %constant_dynamic-update-slice_fusion, bf16[256,4,64,1]{2,1,0,3:T(4,128)(2,1)S(1)} %copy-done.48), kind=kOutput, calls=%fused_computation.1 | convolution fusion | flops 6422528 | bytes 6754304 | tf_op jit(solution)/shard_map/nhd,snhd->hsn/dot_general | solution.py:98
  256.4 5.1 %copy.36 = f32[256,4,49]{1,0,2:T(8,128)} copy(f32[256,4,49]{0,1,2:T(4,128)} %bitcast_convert_fusion) | data formatting | bytes 401408
  261.5 1.8 stack.402
  266.9 1.8 stack.404
  270.5 1.8 stack.814
  274.1 1.8 stack.816
  275.9 1.8 stack.817
  277.6 1.8 stack.818
  279.4 1.8 stack.820
  288.4 1.8 stack.825
  293.7 1.8 stack.829
  295.5 1.8 stack.830
  299.1 1.8 stack.832
  309.8 1.8 stack.839
  311.6 1.8 stack.841
  315.2 1.8 stack.843
  317.0 1.8 stack.844
  324.1 1.8 stack.849
  325.9 1.8 stack.850
  327.7 1.8 stack.851
  337.6 1.9 constant_dynamic-update-slice_fusion.96
  398.0 18.4 %multiply_reduce_fusion = bf16[256,4,64]{2,1,0:T(4,128)(2,1)S(1)} fusion(f32[256,4,49]{1,0,2:T(8,128)} %copy.36, bf16[49,256,4,64]{3,2,1,0:T(4,128)(2,1)} %constant_dynamic-update-slice_fusion.49), kind=kLoop, calls=%fused_computation | loop fusion | flops 9568256 | bytes 6754304
  418.4 2.1 convert_reduce_fusion
  422.1 3.7 fusion.61
  426.2 2.4 stack.859
  429.2 8.0 %reduce.30 = bf16[256,2048]{1,0:T(8,128)(2,1)S(1)} reduce(bf16[256,1,2048]{2,1,0:T(2,128)(2,1)} %stack.859, bf16[]{:T(256)} %broadcast.205), dimensions={1}, to_apply=%stack.859.reduce_sub_computation | reduce | bytes 2097154 | tf_op jit(solution)/shard_map/stack | solution.py:132
  438.8 15.0 %all-to-all-start = ((bf16[256,2,1024]{2,1,0:T(2,128)(2,1)}), bf16[256,2,1024]{2,1,0:T(2,128)(2,1)S(1)}, u32[]{:S(2)}, u32[]{:S(2)}) async-start(bf16[256,2,1024]{2,1,0:T(2,128)(2,1)} %reshape.621), calls=%async_computation | async-start | bytes 2097152 | tf_op jit(solution)/shard_map/all_to_all | solution.py:132
  454.2 31.3 %all-to-all-done = bf16[256,2,1024]{2,1,0:T(2,128)(2,1)S(1)} async-done(((bf16[256,2,1024]{2,1,0:T(2,128)(2,1)}), bf16[256,2,1024]{2,1,0:T(2,128)(2,1)S(1)}, u32[]{:S(2)}, u32[]{:S(2)}) %all-to-all-start) | async-done | bytes 1048608 | tf_op jit(solution)/shard_map/all_to_all | solution.py:132
  485.5 3.3 reshape.622
  488.8 2.2 copy.55
  (384 shorter events, 274.3 us)
Async XLA Ops:
  0.6 493.7 %copy-start = (bf16[1024,1024]{1,0:T(8,128)(2,1)S(1)}, bf16[1024,1024]{1,0:T(8,128)(2,1)}, u32[]{:S(2)}) copy-start(bf16[1024,1024]{1,0:T(8,128)(2,1)} %param.25) | copy-start | bytes 6291460
  11.3 50.3 %collective-permute-start.1 = (bf16[3,16,512]{2,1,0:T(8,128)(2,1)}, bf16[3,16,512]{2,1,0:T(8,128)(2,1)}, u32[]{:S(2)}, u32[]{:S(2)}) collective-permute-start(bf16[3,16,512]{2,1,0:T(8,128)(2,1)} %get-tuple-element.115), channel_id=1, source_target_pairs={{16,0},{32,16},{48,32},{64,48},{80,64},{96,80},{112,96},{128,112},... | collective-permute-start | bytes 147464 | tf_op jit(solution)/shard_map/ppermute | solution.py:23
  16.4 45.2 %collective-permute-start = (bf16[3,16,512]{2,1,0:T(8,128)(2,1)}, bf16[3,16,512]{2,1,0:T(8,128)(2,1)}, u32[]{:S(2)}, u32[]{:S(2)}) collective-permute-start(bf16[3,16,512]{2,1,0:T(8,128)(2,1)} %get-tuple-element.114), channel_id=1, source_target_pairs={{0,16},{16,32},{32,48},{48,64},{64,80},{80,96},{96,112},{112,128},... | collective-permute-start | bytes 147464 | tf_op jit(solution)/shard_map/ppermute | solution.py:21
  63.1 20.8 %collective-permute-start.3 = (bf16[22,3,512]{2,1,0:T(4,128)(2,1)}, bf16[22,3,512]{2,1,0:T(4,128)(2,1)}, u32[]{:S(2)}, u32[]{:S(2)}) collective-permute-start(bf16[22,3,512]{2,1,0:T(4,128)(2,1)} %get-tuple-element.98), channel_id=1, source_target_pairs={{1,0},{2,1},{3,2},{4,3},{5,4},{6,5},{7,6},{8,7},{9,8},{10,9},{11,1... | collective-permute-start | bytes 202760 | tf_op jit(solution)/shard_map/ppermute | solution.py:23
  64.4 19.5 %collective-permute-start.2 = (bf16[22,3,512]{2,1,0:T(4,128)(2,1)}, bf16[22,3,512]{2,1,0:T(4,128)(2,1)}, u32[]{:S(2)}, u32[]{:S(2)}) collective-permute-start(bf16[22,3,512]{2,1,0:T(4,128)(2,1)} %get-tuple-element.99), channel_id=1, source_target_pairs={{0,1},{1,2},{2,3},{3,4},{4,5},{5,6},{6,7},{7,8},{8,9},{9,10},{10,1... | collective-permute-start | bytes 202760 | tf_op jit(solution)/shard_map/ppermute | solution.py:21
  107.2 102.1 %copy-start.3 = (bf16[1,256,4,64]{3,2,1,0:T(4,128)(2,1)S(1)}, bf16[1,256,4,64]{3,2,1,0:T(4,128)(2,1)}, u32[]{:S(2)}) copy-start(bf16[1,256,4,64]{3,2,1,0:T(4,128)(2,1)} %stack.376) | copy-start | bytes 393220
  168.2 43.6 %copy-start.46 = (bf16[1,256,4,64]{3,2,1,0:T(4,128)(2,1)S(1)}, bf16[1,256,4,64]{3,2,1,0:T(4,128)(2,1)}, u32[]{:S(2)}) copy-start(bf16[1,256,4,64]{3,2,1,0:T(4,128)(2,1)} %stack.378) | copy-start | bytes 393220
  168.2 44.4 %copy-start.45 = (bf16[1,256,4,64]{3,2,1,0:T(4,128)(2,1)S(1)}, bf16[1,256,4,64]{3,2,1,0:T(4,128)(2,1)}, u32[]{:S(2)}) copy-start(bf16[1,256,4,64]{3,2,1,0:T(4,128)(2,1)} %stack.379) | copy-start | bytes 393220
  168.2 45.3 %copy-start.43 = (bf16[1,256,4,64]{3,2,1,0:T(4,128)(2,1)S(1)}, bf16[1,256,4,64]{3,2,1,0:T(4,128)(2,1)}, u32[]{:S(2)}) copy-start(bf16[1,256,4,64]{3,2,1,0:T(4,128)(2,1)} %stack.380) | copy-start | bytes 393220
  168.2 46.1 %copy-start.41 = (bf16[1,256,4,64]{3,2,1,0:T(4,128)(2,1)S(1)}, bf16[1,256,4,64]{3,2,1,0:T(4,128)(2,1)}, u32[]{:S(2)}) copy-start(bf16[1,256,4,64]{3,2,1,0:T(4,128)(2,1)} %stack.381) | copy-start | bytes 393220
  168.2 46.9 %copy-start.39 = (bf16[1,256,4,64]{3,2,1,0:T(4,128)(2,1)S(1)}, bf16[1,256,4,64]{3,2,1,0:T(4,128)(2,1)}, u32[]{:S(2)}) copy-start(bf16[1,256,4,64]{3,2,1,0:T(4,128)(2,1)} %stack.382) | copy-start | bytes 393220
  168.2 47.6 %copy-start.6 = (bf16[1,256,4,64]{3,2,1,0:T(4,128)(2,1)S(1)}, bf16[1,256,4,64]{3,2,1,0:T(4,128)(2,1)}, u32[]{:S(2)}) copy-start(bf16[1,256,4,64]{3,2,1,0:T(4,128)(2,1)} %stack.383) | copy-start | bytes 393220
  168.2 48.4 %copy-start.36 = (bf16[1,256,4,64]{3,2,1,0:T(4,128)(2,1)S(1)}, bf16[1,256,4,64]{3,2,1,0:T(4,128)(2,1)}, u32[]{:S(2)}) copy-start(bf16[1,256,4,64]{3,2,1,0:T(4,128)(2,1)} %stack.384) | copy-start | bytes 393220
  168.2 49.2 %copy-start.35 = (bf16[1,256,4,64]{3,2,1,0:T(4,128)(2,1)S(1)}, bf16[1,256,4,64]{3,2,1,0:T(4,128)(2,1)}, u32[]{:S(2)}) copy-start(bf16[1,256,4,64]{3,2,1,0:T(4,128)(2,1)} %stack.385) | copy-start | bytes 393220
  168.2 50.0 %copy-start.33 = (bf16[1,256,4,64]{3,2,1,0:T(4,128)(2,1)S(1)}, bf16[1,256,4,64]{3,2,1,0:T(4,128)(2,1)}, u32[]{:S(2)}) copy-start(bf16[1,256,4,64]{3,2,1,0:T(4,128)(2,1)} %stack.386) | copy-start | bytes 393220
  168.2 50.8 %copy-start.31 = (bf16[1,256,4,64]{3,2,1,0:T(4,128)(2,1)S(1)}, bf16[1,256,4,64]{3,2,1,0:T(4,128)(2,1)}, u32[]{:S(2)}) copy-start(bf16[1,256,4,64]{3,2,1,0:T(4,128)(2,1)} %stack.387) | copy-start | bytes 393220
  168.2 51.6 %copy-start.29 = (bf16[1,256,4,64]{3,2,1,0:T(4,128)(2,1)S(1)}, bf16[1,256,4,64]{3,2,1,0:T(4,128)(2,1)}, u32[]{:S(2)}) copy-start(bf16[1,256,4,64]{3,2,1,0:T(4,128)(2,1)} %stack.388) | copy-start | bytes 393220
  168.2 52.4 %copy-start.27 = (bf16[1,256,4,64]{3,2,1,0:T(4,128)(2,1)S(1)}, bf16[1,256,4,64]{3,2,1,0:T(4,128)(2,1)}, u32[]{:S(2)}) copy-start(bf16[1,256,4,64]{3,2,1,0:T(4,128)(2,1)} %stack.389) | copy-start | bytes 393220
  168.3 53.2 %copy-start.5 = (bf16[1,256,4,64]{3,2,1,0:T(4,128)(2,1)S(1)}, bf16[1,256,4,64]{3,2,1,0:T(4,128)(2,1)}, u32[]{:S(2)}) copy-start(bf16[1,256,4,64]{3,2,1,0:T(4,128)(2,1)} %stack.390) | copy-start | bytes 393220
  168.3 54.0 %copy-start.24 = (bf16[1,256,4,64]{3,2,1,0:T(4,128)(2,1)S(1)}, bf16[1,256,4,64]{3,2,1,0:T(4,128)(2,1)}, u32[]{:S(2)}) copy-start(bf16[1,256,4,64]{3,2,1,0:T(4,128)(2,1)} %stack.391) | copy-start | bytes 393220
  168.3 54.8 %copy-start.23 = (bf16[1,256,4,64]{3,2,1,0:T(4,128)(2,1)S(1)}, bf16[1,256,4,64]{3,2,1,0:T(4,128)(2,1)}, u32[]{:S(2)}) copy-start(bf16[1,256,4,64]{3,2,1,0:T(4,128)(2,1)} %stack.392) | copy-start | bytes 393220
  168.3 55.6 %copy-start.21 = (bf16[1,256,4,64]{3,2,1,0:T(4,128)(2,1)S(1)}, bf16[1,256,4,64]{3,2,1,0:T(4,128)(2,1)}, u32[]{:S(2)}) copy-start(bf16[1,256,4,64]{3,2,1,0:T(4,128)(2,1)} %stack.393) | copy-start | bytes 393220
  168.3 56.4 %copy-start.19 = (bf16[1,256,4,64]{3,2,1,0:T(4,128)(2,1)S(1)}, bf16[1,256,4,64]{3,2,1,0:T(4,128)(2,1)}, u32[]{:S(2)}) copy-start(bf16[1,256,4,64]{3,2,1,0:T(4,128)(2,1)} %stack.394) | copy-start | bytes 393220
  168.3 57.2 %copy-start.17 = (bf16[1,256,4,64]{3,2,1,0:T(4,128)(2,1)S(1)}, bf16[1,256,4,64]{3,2,1,0:T(4,128)(2,1)}, u32[]{:S(2)}) copy-start(bf16[1,256,4,64]{3,2,1,0:T(4,128)(2,1)} %stack.395) | copy-start | bytes 393220
  168.3 58.0 %copy-start.15 = (bf16[1,256,4,64]{3,2,1,0:T(4,128)(2,1)S(1)}, bf16[1,256,4,64]{3,2,1,0:T(4,128)(2,1)}, u32[]{:S(2)}) copy-start(bf16[1,256,4,64]{3,2,1,0:T(4,128)(2,1)} %stack.396) | copy-start | bytes 393220
  168.3 58.8 %copy-start.4 = (bf16[1,256,4,64]{3,2,1,0:T(4,128)(2,1)S(1)}, bf16[1,256,4,64]{3,2,1,0:T(4,128)(2,1)}, u32[]{:S(2)}) copy-start(bf16[1,256,4,64]{3,2,1,0:T(4,128)(2,1)} %stack.397) | copy-start | bytes 393220
  168.3 59.6 %copy-start.12 = (bf16[1,256,4,64]{3,2,1,0:T(4,128)(2,1)S(1)}, bf16[1,256,4,64]{3,2,1,0:T(4,128)(2,1)}, u32[]{:S(2)}) copy-start(bf16[1,256,4,64]{3,2,1,0:T(4,128)(2,1)} %stack.398) | copy-start | bytes 393220
  168.3 60.4 %copy-start.10 = (bf16[1,256,4,64]{3,2,1,0:T(4,128)(2,1)S(1)}, bf16[1,256,4,64]{3,2,1,0:T(4,128)(2,1)}, u32[]{:S(2)}) copy-start(bf16[1,256,4,64]{3,2,1,0:T(4,128)(2,1)} %stack.399) | copy-start | bytes 393220
  168.4 61.2 %copy-start.7 = (bf16[1,256,4,64]{3,2,1,0:T(4,128)(2,1)S(1)}, bf16[1,256,4,64]{3,2,1,0:T(4,128)(2,1)}, u32[]{:S(2)}) copy-start(bf16[1,256,4,64]{3,2,1,0:T(4,128)(2,1)} %stack.400) | copy-start | bytes 393220
  168.4 62.0 %copy-start.48 = (bf16[256,4,64,1]{2,1,0,3:T(4,128)(2,1)S(1)}, bf16[256,4,64,1]{2,1,0,3:T(4,128)(2,1)}, u32[]{:S(2)}) copy-start(bf16[256,4,64,1]{2,1,0,3:T(4,128)(2,1)} %fusion.22) | copy-start | bytes 393220
  227.1 28.0 %copy-start.50 = (f32[4]{0:T(128)S(1)}, f32[4]{0:T(128)}, u32[]{:S(2)}) copy-start(f32[4]{0:T(128)} %broadcast_multiply_fusion.1) | copy-start | bytes 52
  261.5 104.2 %copy-start.2 = (bf16[1,256,4,64]{3,2,1,0:T(4,128)(2,1)S(1)}, bf16[1,256,4,64]{3,2,1,0:T(4,128)(2,1)}, u32[]{:S(2)}) copy-start(bf16[1,256,4,64]{3,2,1,0:T(4,128)(2,1)} %stack.826) | copy-start | bytes 393220
  337.5 42.0 %copy-start.44 = (bf16[1,256,4,64]{3,2,1,0:T(4,128)(2,1)S(1)}, bf16[1,256,4,64]{3,2,1,0:T(4,128)(2,1)}, u32[]{:S(2)}) copy-start(bf16[1,256,4,64]{3,2,1,0:T(4,128)(2,1)} %stack.835) | copy-start | bytes 393220
  337.5 42.8 %copy-start.42 = (bf16[1,256,4,64]{3,2,1,0:T(4,128)(2,1)S(1)}, bf16[1,256,4,64]{3,2,1,0:T(4,128)(2,1)}, u32[]{:S(2)}) copy-start(bf16[1,256,4,64]{3,2,1,0:T(4,128)(2,1)} %stack.836) | copy-start | bytes 393220
  337.5 43.6 %copy-start.40 = (bf16[1,256,4,64]{3,2,1,0:T(4,128)(2,1)S(1)}, bf16[1,256,4,64]{3,2,1,0:T(4,128)(2,1)}, u32[]{:S(2)}) copy-start(bf16[1,256,4,64]{3,2,1,0:T(4,128)(2,1)} %stack.837) | copy-start | bytes 393220
  337.5 44.5 %copy-start.38 = (bf16[1,256,4,64]{3,2,1,0:T(4,128)(2,1)S(1)}, bf16[1,256,4,64]{3,2,1,0:T(4,128)(2,1)}, u32[]{:S(2)}) copy-start(bf16[1,256,4,64]{3,2,1,0:T(4,128)(2,1)} %stack.838) | copy-start | bytes 393220
  337.5 45.2 %copy-start.37 = (bf16[1,256,4,64]{3,2,1,0:T(4,128)(2,1)S(1)}, bf16[1,256,4,64]{3,2,1,0:T(4,128)(2,1)}, u32[]{:S(2)}) copy-start(bf16[1,256,4,64]{3,2,1,0:T(4,128)(2,1)} %stack.839) | copy-start | bytes 393220
  337.5 46.9 %copy-start.34 = (bf16[1,256,4,64]{3,2,1,0:T(4,128)(2,1)S(1)}, bf16[1,256,4,64]{3,2,1,0:T(4,128)(2,1)}, u32[]{:S(2)}) copy-start(bf16[1,256,4,64]{3,2,1,0:T(4,128)(2,1)} %stack.841) | copy-start | bytes 393220
  337.5 47.6 %copy-start.32 = (bf16[1,256,4,64]{3,2,1,0:T(4,128)(2,1)S(1)}, bf16[1,256,4,64]{3,2,1,0:T(4,128)(2,1)}, u32[]{:S(2)}) copy-start(bf16[1,256,4,64]{3,2,1,0:T(4,128)(2,1)} %stack.842) | copy-start | bytes 393220
  337.5 48.4 %copy-start.30 = (bf16[1,256,4,64]{3,2,1,0:T(4,128)(2,1)S(1)}, bf16[1,256,4,64]{3,2,1,0:T(4,128)(2,1)}, u32[]{:S(2)}) copy-start(bf16[1,256,4,64]{3,2,1,0:T(4,128)(2,1)} %stack.843) | copy-start | bytes 393220
  337.5 49.2 %copy-start.28 = (bf16[1,256,4,64]{3,2,1,0:T(4,128)(2,1)S(1)}, bf16[1,256,4,64]{3,2,1,0:T(4,128)(2,1)}, u32[]{:S(2)}) copy-start(bf16[1,256,4,64]{3,2,1,0:T(4,128)(2,1)} %stack.844) | copy-start | bytes 393220
  337.5 50.0 %copy-start.26 = (bf16[1,256,4,64]{3,2,1,0:T(4,128)(2,1)S(1)}, bf16[1,256,4,64]{3,2,1,0:T(4,128)(2,1)}, u32[]{:S(2)}) copy-start(bf16[1,256,4,64]{3,2,1,0:T(4,128)(2,1)} %stack.845) | copy-start | bytes 393220
  337.5 50.8 %copy-start.25 = (bf16[1,256,4,64]{3,2,1,0:T(4,128)(2,1)S(1)}, bf16[1,256,4,64]{3,2,1,0:T(4,128)(2,1)}, u32[]{:S(2)}) copy-start(bf16[1,256,4,64]{3,2,1,0:T(4,128)(2,1)} %stack.846) | copy-start | bytes 393220
  337.5 52.4 %copy-start.22 = (bf16[1,256,4,64]{3,2,1,0:T(4,128)(2,1)S(1)}, bf16[1,256,4,64]{3,2,1,0:T(4,128)(2,1)}, u32[]{:S(2)}) copy-start(bf16[1,256,4,64]{3,2,1,0:T(4,128)(2,1)} %stack.848) | copy-start | bytes 393220
  337.6 53.2 %copy-start.20 = (bf16[1,256,4,64]{3,2,1,0:T(4,128)(2,1)S(1)}, bf16[1,256,4,64]{3,2,1,0:T(4,128)(2,1)}, u32[]{:S(2)}) copy-start(bf16[1,256,4,64]{3,2,1,0:T(4,128)(2,1)} %stack.849) | copy-start | bytes 393220
  337.6 53.9 %copy-start.18 = (bf16[1,256,4,64]{3,2,1,0:T(4,128)(2,1)S(1)}, bf16[1,256,4,64]{3,2,1,0:T(4,128)(2,1)}, u32[]{:S(2)}) copy-start(bf16[1,256,4,64]{3,2,1,0:T(4,128)(2,1)} %stack.850) | copy-start | bytes 393220
  337.6 54.8 %copy-start.16 = (bf16[1,256,4,64]{3,2,1,0:T(4,128)(2,1)S(1)}, bf16[1,256,4,64]{3,2,1,0:T(4,128)(2,1)}, u32[]{:S(2)}) copy-start(bf16[1,256,4,64]{3,2,1,0:T(4,128)(2,1)} %stack.851) | copy-start | bytes 393220
  337.6 55.6 %copy-start.13 = (bf16[1,256,4,64]{3,2,1,0:T(4,128)(2,1)S(1)}, bf16[1,256,4,64]{3,2,1,0:T(4,128)(2,1)}, u32[]{:S(2)}) copy-start(bf16[1,256,4,64]{3,2,1,0:T(4,128)(2,1)} %stack.852) | copy-start | bytes 393220
  337.6 56.4 %copy-start.14 = (bf16[1,256,4,64]{3,2,1,0:T(4,128)(2,1)S(1)}, bf16[1,256,4,64]{3,2,1,0:T(4,128)(2,1)}, u32[]{:S(2)}) copy-start(bf16[1,256,4,64]{3,2,1,0:T(4,128)(2,1)} %stack.853) | copy-start | bytes 393220
  337.6 58.0 %copy-start.11 = (bf16[1,256,4,64]{3,2,1,0:T(4,128)(2,1)S(1)}, bf16[1,256,4,64]{3,2,1,0:T(4,128)(2,1)}, u32[]{:S(2)}) copy-start(bf16[1,256,4,64]{3,2,1,0:T(4,128)(2,1)} %stack.855) | copy-start | bytes 393220
  337.6 58.8 %copy-start.8 = (bf16[1,256,4,64]{3,2,1,0:T(4,128)(2,1)S(1)}, bf16[1,256,4,64]{3,2,1,0:T(4,128)(2,1)}, u32[]{:S(2)}) copy-start(bf16[1,256,4,64]{3,2,1,0:T(4,128)(2,1)} %stack.856) | copy-start | bytes 393220
  337.6 59.6 %copy-start.9 = (bf16[1,256,4,64]{3,2,1,0:T(4,128)(2,1)S(1)}, bf16[1,256,4,64]{3,2,1,0:T(4,128)(2,1)}, u32[]{:S(2)}) copy-start(bf16[1,256,4,64]{3,2,1,0:T(4,128)(2,1)} %stack.857) | copy-start | bytes 393220
  389.1 27.4 %copy-start.1 = (bf16[16,16,256]{2,1,0:T(8,128)(2,1)S(1)}, bf16[16,16,256]{2,1,0:T(8,128)(2,1)}, u32[]{:S(2)}) copy-start(bf16[16,16,256]{2,1,0:T(8,128)(2,1)} %param.13) | copy-start | bytes 393220
  389.1 27.4 %copy-start.49 = (bf16[256,256]{1,0:T(8,128)(2,1)S(1)}, bf16[256,256]{1,0:T(8,128)(2,1)}, u32[]{:S(2)}) copy-start(bf16[256,256]{1,0:T(8,128)(2,1)} %param.17) | copy-start | bytes 393220
  389.9 27.0 %copy-start.52 = (f32[256]{0:T(256)S(1)}, f32[256]{0:T(256)}, u32[]{:S(2)}) copy-start(f32[256]{0:T(256)} %param.18) | copy-start | bytes 3076
  398.0 22.6 %copy-start.47 = (bf16[256,1024]{1,0:T(8,128)(2,1)S(1)}, bf16[256,1024]{1,0:T(8,128)(2,1)}, u32[]{:S(2)}) copy-start(bf16[256,1024]{1,0:T(8,128)(2,1)} %param.21) | copy-start | bytes 1572868
  398.0 24.0 %copy-start.51 = (f32[1024]{0:T(1024)S(1)}, f32[1024]{0:T(1024)}, u32[]{:S(2)}) copy-start(f32[1024]{0:T(1024)} %param.22) | copy-start | bytes 12292
  416.4 37.4 %copy-start.53 = (f32[16]{0:T(128)S(1)}, f32[16]{0:T(128)}, u32[]{:S(2)}) copy-start(f32[16]{0:T(128)} %param.24) | copy-start | bytes 196
  438.8 46.7 %all-to-all-start = ((bf16[256,2,1024]{2,1,0:T(2,128)(2,1)}), bf16[256,2,1024]{2,1,0:T(2,128)(2,1)S(1)}, u32[]{:S(2)}, u32[]{:S(2)}) async-start(bf16[256,2,1024]{2,1,0:T(2,128)(2,1)} %reshape.621), calls=%async_computation | async-start | bytes 2097152 | tf_op jit(solution)/shard_map/all_to_all | solution.py:132
